TPU v7x, 32 devices: a whole 2x2x4 slice. The times are simulated.
32 devices in a mesh: dp: 2 (over core), ctx: 4 (over z), fsdp: 4 (over y, x).
Axes of the slice: x: 2, y: 2, z: 4, core: 2. Of those that a mesh axis runs over, the one named last changes fastest.
Arguments:
- tokens: bfloat16 [8, 2, 1024, 2048], P(('dp', 'fsdp'), None, 'ctx'), may hold values from -6 to 6
- cotangent: bfloat16 [8, 2, 1024, 2048], P(('dp', 'fsdp'), None, 'ctx'), may hold values from -6 to 6
- lengths: int32 [8, 2], P(('dp', 'fsdp')), may hold values from 513 to 1024, as said below
- deal: int32 [8, 2, 8], P(('dp', 'fsdp')), may hold values from 0 to 7, each once within a row
- ln_gain: bfloat16 [2048], P('fsdp'), may hold values from 0.5 to 1.5
- ln_bias: bfloat16 [2048], P('fsdp'), may hold values from -1 to 1
- w_qkv: bfloat16 [2048, 6144], P('fsdp'), may hold values from -0.125 to 0.125
- b_qkv: bfloat16 [6144], P('fsdp'), may hold values from -1 to 1
- w_out: bfloat16 [2048, 2048], P('fsdp'), may hold values from -3 to 3
- b_out: bfloat16 [2048], P('fsdp'), may hold values from -2.5 to 2.5
- w_up: bfloat16 [2048, 8192], P('fsdp'), may hold values from -0.125 to 0.125
- b_up: bfloat16 [8192], P('fsdp'), may hold values from -1 to 1
- w_down: bfloat16 [8192, 2048], P('fsdp'), may hold values from -0.0625 to 0.0625
- b_down: bfloat16 [2048], P('fsdp'), may hold values from -2.5 to 2.5
Outputs:
- outputs: bfloat16 [8, 2, 1024, 2048], P(('dp', 'fsdp'), None, 'ctx')
- input_grad: bfloat16 [8, 2, 1024, 2048], P(('dp', 'fsdp'), None, 'ctx')
- grad_ln_gain: float32 [2048], P('fsdp')
- grad_ln_bias: float32 [2048], P('fsdp')
- grad_w_qkv: float32 [2048, 6144], P('fsdp')
- grad_b_qkv: float32 [6144], P('fsdp')
- grad_w_out: float32 [2048, 2048], P('fsdp')
- grad_b_out: float32 [2048], P('fsdp')
- grad_w_up: float32 [2048, 8192], P('fsdp')
- grad_b_up: float32 [8192], P('fsdp')
- grad_w_down: float32 [8192, 2048], P('fsdp')
- grad_b_down: float32 [2048], P('fsdp')
Inputs may be any that keep to these rules, and one draw needn't show every extreme that they name: lengths[g, m] tokens fill the first positions of a sequence, the rest is padding; in every draw one sequence is exactly 1024 long and one exactly 513. Each row of deal is a permutation of the 8 blocks of a sequence.
All inputs are finite; a program needn't handle non-finite values.
Results may differ from a plain program's by a relative error of at most 0.02.
Values may be sent and summed in bfloat16 or wider, within the bound.
No kernel may reach another device: no remote copies, remote signals or barrier semaphores. Data moves between devices by JAX's collectives and lax.ppermute only.
A program may use at most 832 MiB of HBM per device.

v0:
```python
import jax
import jax.numpy as jnp
from jax import lax
from jax.sharding import PartitionSpec as P

HEAD_DIM = 64
ROT = 32
EPS = 1e-05
BASE = 10000.0


def contract_rows(left, right):
    return lax.dot_general(
        left, right, (((0,), (0,)), ((), ())), preferred_element_type=jnp.float32
    )


def contract_cols(left, right):
    return lax.dot_general(
        left, right, (((1,), (1,)), ((), ())), preferred_element_type=jnp.float32
    )


def angles_of(positions):
    half = ROT // 2
    freqs = BASE ** (-(jnp.arange(half, dtype=jnp.float32) * 2.0) / ROT)
    angles = positions.astype(jnp.float32)[:, None] * freqs[None, :]
    return (jnp.cos(angles)[:, None, :], jnp.sin(angles)[:, None, :])


def rotate(values, cosine, sine):
    half = ROT // 2
    first = values[..., :half]
    second = values[..., half:ROT]
    return jnp.concatenate(
        [first * cosine - second * sine, second * cosine + first * sine, values[..., ROT:]], axis=-1
    )


def rotate_back(values, cosine, sine):
    half = ROT // 2
    first = values[..., :half]
    second = values[..., half:ROT]
    return jnp.concatenate(
        [first * cosine + second * sine, second * cosine - first * sine, values[..., ROT:]], axis=-1
    )


def layer_step(weights, inputs, upstream, length, deal_row):
    gain, shift, w_qkv, b_qkv, w_out, b_out, w_up, b_up, w_down, b_down = weights
    row_count, width = inputs.shape
    block_rows = row_count // 2
    head_count = width // HEAD_DIM
    scale = HEAD_DIM ** (-0.5)
    place = lax.axis_index("ctx")
    offsets = jnp.arange(block_rows, dtype=jnp.int32)
    own_blocks = lax.dynamic_slice_in_dim(deal_row, 2 * place, 2)
    local_pos = (own_blocks[:, None] * block_rows + offsets[None, :]).reshape(row_count)
    every_pos = (deal_row[:, None] * block_rows + offsets[None, :]).reshape(-1)
    valid = (local_pos < length).astype(jnp.float32)[:, None]
    allowed = (every_pos[None, :] <= local_pos[:, None]) & (every_pos[None, :] < length)
    cosine, sine = angles_of(local_pos)
    inputs_f = inputs.astype(jnp.float32)
    gain_f = gain.astype(jnp.float32)
    centered = inputs_f - jnp.mean(inputs_f, axis=-1, keepdims=True)
    variance = jnp.mean(centered * centered, axis=-1, keepdims=True)
    inv_std = lax.rsqrt(variance + EPS)
    normed = centered * inv_std
    hidden = (normed * gain_f + shift.astype(jnp.float32)).astype(jnp.bfloat16)
    joined = jnp.dot(hidden, w_qkv, preferred_element_type=jnp.float32) + b_qkv.astype(jnp.float32)
    query = (
        rotate(joined[:, :width].reshape(row_count, head_count, HEAD_DIM), cosine, sine)
        .reshape(row_count, width)
        .astype(jnp.bfloat16)
    )
    keyed = (
        rotate(joined[:, width : 2 * width].reshape(row_count, head_count, HEAD_DIM), cosine, sine)
        .reshape(row_count, width)
        .astype(jnp.bfloat16)
    )
    valued = joined[:, 2 * width :].astype(jnp.bfloat16)
    keys_all, values_all = (
        lax.all_gather(keyed, "ctx", axis=0, tiled=True),
        lax.all_gather(valued, "ctx", axis=0, tiled=True),
    )
    total_keys = keys_all.shape[0]
    group = min(8, head_count)
    span = group * HEAD_DIM

    def heads_of(array, start, count):
        return array[:, start : start + span].reshape(count, group, HEAD_DIM)

    def block_scores(start):
        raw = (
            jnp.einsum(
                "qhd,khd->hqk",
                heads_of(query, start, row_count),
                heads_of(keys_all, start, total_keys),
                preferred_element_type=jnp.float32,
            )
            * scale
        )
        return jnp.where(allowed[None], raw, -1e30)

    attended_parts = []
    lse_parts = []
    for start in range(0, width, span):
        masked = block_scores(start)
        highest = jnp.max(masked, axis=-1, keepdims=True)
        expo = jnp.exp(masked - highest)
        total = jnp.sum(expo, axis=-1, keepdims=True)
        weights_low = (expo / total).astype(jnp.bfloat16)
        mixed = jnp.einsum(
            "hqk,khd->qhd",
            weights_low,
            heads_of(values_all, start, total_keys),
            preferred_element_type=jnp.float32,
        )
        attended_parts.append(mixed.reshape(row_count, span))
        lse_parts.append(highest + jnp.log(total))
    attended = jnp.concatenate(attended_parts, axis=1).astype(jnp.bfloat16)
    branch = jnp.dot(attended, w_out, preferred_element_type=jnp.float32) + b_out.astype(
        jnp.float32
    )
    upward = jnp.dot(hidden, w_up, preferred_element_type=jnp.float32) + b_up.astype(jnp.float32)
    activated = jax.nn.gelu(upward, approximate=True).astype(jnp.bfloat16)
    feed = jnp.dot(activated, w_down, preferred_element_type=jnp.float32) + b_down.astype(
        jnp.float32
    )
    result = (valid * (inputs_f + branch + feed)).astype(jnp.bfloat16)
    grad_out = upstream.astype(jnp.float32) * valid
    grad_low = grad_out.astype(jnp.bfloat16)
    row_total = jnp.sum(grad_out, axis=0)
    d_down = contract_rows(activated, grad_low)
    d_wout = contract_rows(attended, grad_low)
    d_act = contract_cols(grad_low, w_down)
    _, gelu_pull = jax.vjp(lambda value: jax.nn.gelu(value, approximate=True), upward)
    d_upward = gelu_pull(d_act)[0].astype(jnp.bfloat16)
    d_wup = contract_rows(hidden, d_upward)
    d_bup = jnp.sum(d_upward.astype(jnp.float32), axis=0)
    d_attended = contract_cols(grad_low, w_out).astype(jnp.bfloat16)
    dq_parts = []
    dk_parts = []
    dv_parts = []
    delta_parts = []
    for index, start in enumerate(range(0, width, span)):
        masked = block_scores(start)
        probs = jnp.where(allowed[None], jnp.exp(masked - lse_parts[index]), 0.0)
        d_heads = heads_of(d_attended, start, row_count)
        d_probs = jnp.einsum(
            "qhd,khd->hqk",
            d_heads,
            heads_of(values_all, start, total_keys),
            preferred_element_type=jnp.float32,
        )
        delta = jnp.sum(probs * d_probs, axis=-1, keepdims=True)
        d_scores = (probs * (d_probs - delta)).astype(jnp.bfloat16)
        d_query = (
            jnp.einsum(
                "hqk,khd->qhd",
                d_scores,
                heads_of(keys_all, start, total_keys),
                preferred_element_type=jnp.float32,
            )
            * scale
        )
        dq_parts.append(d_query.reshape(row_count, span))
        delta_parts.append(delta[:, :, 0].T)
        d_keyed = (
            jnp.einsum(
                "hqk,qhd->khd",
                d_scores,
                heads_of(query, start, row_count),
                preferred_element_type=jnp.float32,
            )
            * scale
        )
        d_valued = jnp.einsum(
            "hqk,qhd->khd", probs.astype(jnp.bfloat16), d_heads, preferred_element_type=jnp.float32
        )
        dk_parts.append(d_keyed.reshape(total_keys, span))
        dv_parts.append(d_valued.reshape(total_keys, span))
    keys_grad_all = jnp.concatenate(dk_parts, axis=1)
    values_grad_all = jnp.concatenate(dv_parts, axis=1)
    keys_grad, values_grad = (
        lax.psum_scatter(
            keys_grad_all.astype(jnp.bfloat16), "ctx", scatter_dimension=0, tiled=True
        ).astype(jnp.float32),
        lax.psum_scatter(
            values_grad_all.astype(jnp.bfloat16), "ctx", scatter_dimension=0, tiled=True
        ).astype(jnp.float32),
    )
    query_grad = rotate_back(
        jnp.concatenate(dq_parts, axis=1).reshape(row_count, head_count, HEAD_DIM), cosine, sine
    ).reshape(row_count, width)
    keyed_grad = rotate_back(
        keys_grad.reshape(row_count, head_count, HEAD_DIM), cosine, sine
    ).reshape(row_count, width)
    d_joined = jnp.concatenate([query_grad, keyed_grad, values_grad], axis=1).astype(jnp.bfloat16)
    d_wqkv = contract_rows(hidden, d_joined)
    d_bqkv = jnp.sum(d_joined.astype(jnp.float32), axis=0)
    d_hidden = contract_cols(d_joined, w_qkv) + contract_cols(d_upward, w_up)
    d_gain = jnp.sum(d_hidden * normed, axis=0)
    d_shift = jnp.sum(d_hidden, axis=0)
    d_norm = d_hidden * gain_f
    d_inputs = inv_std * (
        d_norm
        - jnp.mean(d_norm, axis=-1, keepdims=True)
        - normed * jnp.mean(d_norm * normed, axis=-1, keepdims=True)
    )
    back = (grad_out + d_inputs).astype(jnp.bfloat16)
    return (
        result,
        back,
        (d_gain, d_shift, d_wqkv, d_bqkv, d_wout, row_total, d_wup, d_bup, d_down, row_total),
    )


def body(
    tokens,
    cotangent,
    lengths,
    deal,
    ln_gain,
    ln_bias,
    w_qkv,
    b_qkv,
    w_out,
    b_out,
    w_up,
    b_up,
    w_down,
    b_down,
):
    shards = (ln_gain, ln_bias, w_qkv, b_qkv, w_out, b_out, w_up, b_up, w_down, b_down)
    shard_count = lax.axis_size("fsdp")
    summed = tuple(
        (
            jnp.zeros((piece.shape[0] * shard_count,) + piece.shape[1:], jnp.float32)
            for piece in shards
        )
    )
    results = []
    backs = []
    for micro_index in range(tokens.shape[1]):
        gathered = (
            lax.all_gather(ln_gain, "fsdp", axis=0, tiled=True),
            lax.all_gather(ln_bias, "fsdp", axis=0, tiled=True),
            lax.all_gather(w_qkv, "fsdp", axis=0, tiled=True),
            lax.all_gather(b_qkv, "fsdp", axis=0, tiled=True),
            lax.all_gather(w_out, "fsdp", axis=0, tiled=True),
            lax.all_gather(b_out, "fsdp", axis=0, tiled=True),
            lax.all_gather(w_up, "fsdp", axis=0, tiled=True),
            lax.all_gather(b_up, "fsdp", axis=0, tiled=True),
            lax.all_gather(w_down, "fsdp", axis=0, tiled=True),
            lax.all_gather(b_down, "fsdp", axis=0, tiled=True),
        )
        result, back, local = layer_step(
            gathered,
            tokens[0, micro_index],
            cotangent[0, micro_index],
            lengths[0, micro_index],
            deal[0, micro_index],
        )
        results.append(result)
        backs.append(back)
        summed = tuple((older + newer for older, newer in zip(summed, local)))
    summed = (
        lax.psum_scatter(
            summed[0].astype(jnp.bfloat16), "fsdp", scatter_dimension=0, tiled=True
        ).astype(jnp.float32),
        lax.psum_scatter(
            summed[1].astype(jnp.bfloat16), "fsdp", scatter_dimension=0, tiled=True
        ).astype(jnp.float32),
        lax.psum_scatter(
            summed[2].astype(jnp.bfloat16), "fsdp", scatter_dimension=0, tiled=True
        ).astype(jnp.float32),
        lax.psum_scatter(
            summed[3].astype(jnp.bfloat16), "fsdp", scatter_dimension=0, tiled=True
        ).astype(jnp.float32),
        lax.psum_scatter(
            summed[4].astype(jnp.bfloat16), "fsdp", scatter_dimension=0, tiled=True
        ).astype(jnp.float32),
        lax.psum_scatter(
            summed[5].astype(jnp.bfloat16), "fsdp", scatter_dimension=0, tiled=True
        ).astype(jnp.float32),
        lax.psum_scatter(
            summed[6].astype(jnp.bfloat16), "fsdp", scatter_dimension=0, tiled=True
        ).astype(jnp.float32),
        lax.psum_scatter(
            summed[7].astype(jnp.bfloat16), "fsdp", scatter_dimension=0, tiled=True
        ).astype(jnp.float32),
        lax.psum_scatter(
            summed[8].astype(jnp.bfloat16), "fsdp", scatter_dimension=0, tiled=True
        ).astype(jnp.float32),
        lax.psum_scatter(
            summed[9].astype(jnp.bfloat16), "fsdp", scatter_dimension=0, tiled=True
        ).astype(jnp.float32),
    )
    totals = (
        lax.psum(summed[0].astype(jnp.bfloat16), ("dp", "ctx")).astype(jnp.float32),
        lax.psum(summed[1].astype(jnp.bfloat16), ("dp", "ctx")).astype(jnp.float32),
        lax.psum(summed[2].astype(jnp.bfloat16), ("dp", "ctx")).astype(jnp.float32),
        lax.psum(summed[3].astype(jnp.bfloat16), ("dp", "ctx")).astype(jnp.float32),
        lax.psum(summed[4].astype(jnp.bfloat16), ("dp", "ctx")).astype(jnp.float32),
        lax.psum(summed[5].astype(jnp.bfloat16), ("dp", "ctx")).astype(jnp.float32),
        lax.psum(summed[6].astype(jnp.bfloat16), ("dp", "ctx")).astype(jnp.float32),
        lax.psum(summed[7].astype(jnp.bfloat16), ("dp", "ctx")).astype(jnp.float32),
        lax.psum(summed[8].astype(jnp.bfloat16), ("dp", "ctx")).astype(jnp.float32),
        lax.psum(summed[9].astype(jnp.bfloat16), ("dp", "ctx")).astype(jnp.float32),
    )
    stacked_out = jnp.stack(results)[None]
    stacked_back = jnp.stack(backs)[None]
    return (
        stacked_out,
        stacked_back,
        totals[0],
        totals[1],
        totals[2],
        totals[3],
        totals[4],
        totals[5],
        totals[6],
        totals[7],
        totals[8],
        totals[9],
    )


def solution(mesh):
    in_specs = (
        P(("dp", "fsdp"), None, "ctx", None),
        P(("dp", "fsdp"), None, "ctx", None),
        P(("dp", "fsdp"), None),
        P(("dp", "fsdp"), None, None),
        P("fsdp"),
        P("fsdp"),
        P("fsdp", None),
        P("fsdp"),
        P("fsdp", None),
        P("fsdp"),
        P("fsdp", None),
        P("fsdp"),
        P("fsdp", None),
        P("fsdp"),
    )
    out_specs = (
        P(("dp", "fsdp"), None, "ctx", None),
        P(("dp", "fsdp"), None, "ctx", None),
        P("fsdp"),
        P("fsdp"),
        P("fsdp", None),
        P("fsdp"),
        P("fsdp", None),
        P("fsdp"),
        P("fsdp", None),
        P("fsdp"),
        P("fsdp", None),
        P("fsdp"),
    )
    return jax.shard_map(body, mesh=mesh, in_specs=in_specs, out_specs=out_specs, check_vma=False)
```

profile of v0, /device:TPU:0, one launch (start us, length us, event | category | flops | bytes accessed | tf_op | source)
XLA Modules:
  0.0 3160.4 jit_solution(15819114740749781028)
XLA Ops:
  34.9 205.6 %all-gather.14.cloned.1.call-done = bf16[2048,6144]{1,0:T(8,128)(2,1)} async-done(((bf16[512,6144]{1,0:T(8,128)(2,1)}), bf16[2048,6144]{1,0:T(8,128)(2,1)}) %all-gather.14.cloned.1.call-update) | async-done | bytes 25165840 | tf_op jit(solution)/shard_map/all_gather | solution.py:249
  306.2 23.8 all-gather.20.cloned.1.call-done
  358.4 53.9 %all-gather.16.cloned.1.call-done = bf16[1024,2048]{1,0:T(8,128)(2,1)} async-done(((bf16[256,2048]{1,0:T(8,128)(2,1)}), bf16[1024,2048]{1,0:T(8,128)(2,1)}) %all-gather.16.cloned.1.call-update) | async-done | bytes 4194320 | tf_op jit(solution)/shard_map/all_gather | solution.py:84
  423.7 70.0 %all-gather.26.cloned.1.call-done = bf16[1024,2048]{1,0:T(8,128)(2,1)} async-done(((bf16[256,2048]{1,0:T(8,128)(2,1)}), bf16[1024,2048]{1,0:T(8,128)(2,1)}) %all-gather.26.cloned.1.call-update) | async-done | bytes 4194320 | tf_op jit(solution)/shard_map/all_gather | solution.py:84
  498.9 75.3 %all-gather.18.cloned.1.call-done = bf16[1024,2048]{0,1:T(8,128)(2,1)} async-done(((bf16[256,2048]{0,1:T(8,128)(2,1)}), bf16[1024,2048]{0,1:T(8,128)(2,1)}) %all-gather.18.cloned.1.call-update) | async-done | bytes 4194320 | tf_op jit(solution)/shard_map/all_gather | solution.py:83
  586.8 68.1 %all-gather.28.cloned.1.call-done = bf16[1024,2048]{0,1:T(8,128)(2,1)} async-done(((bf16[256,2048]{0,1:T(8,128)(2,1)}), bf16[1024,2048]{0,1:T(8,128)(2,1)}) %all-gather.28.cloned.1.call-update) | async-done | bytes 4194320 | tf_op jit(solution)/shard_map/all_gather | solution.py:83
  742.4 26.8 multiply_convert_fusion.7
  851.1 27.0 multiply_convert_fusion.3
  1014.6 31.2 reduce-scatter.15.cloned.1.call-done
  1066.4 59.6 %reduce-scatter.19.cloned.1.call-done = bf16[256,2048]{0,1:T(8,128)(2,1)} async-done(((bf16[1024,2048]{0,1:T(8,128)(2,1)}), bf16[256,2048]{0,1:T(8,128)(2,1)}) %reduce-scatter.19.cloned.1.call-update) | async-done | bytes 1048592 | tf_op jit(solution)/shard_map/reduce_scatter | solution.py:189
  1126.0 32.0 %add_convert_fusion.2 = bf16[2048,6144]{1,0:T(8,128)(2,1)} fusion(f32[2048,6144]{1,0:T(8,128)} %fusion.190, bf16[256,2048]{0,1:T(8,128)(2,1)} %reduce-scatter.19.cloned.1.call-done, bf16[256,2048]{0,1:T(8,128)(2,1)} %bitcast.429, bf16[256,2048]{0,1:T(8,128)(2,1)S(1)} %bitcast.426, f32[256]{0:T(256)S(1)} %copy-done.110, f32[256]{0:T(256)S(1)} %copy-done.107, ...), kind=kOutput, calls=%fused_computation.2 | convolution fusion | flops 6480199680 | bytes 79710208 | tf_op jit(solution)/shard_map/dot_general | solution.py:13
  1167.1 258.5 %all-gather.22.cloned.1.call-done = bf16[2048,8192]{1,0:T(8,128)(2,1)} async-done(((bf16[512,8192]{1,0:T(8,128)(2,1)}), bf16[2048,8192]{1,0:T(8,128)(2,1)}) %all-gather.22.cloned.1.call-update) | async-done | bytes 33554448 | tf_op jit(solution)/shard_map/all_gather | solution.py:253
  1466.3 258.3 %all-gather.24.cloned.1.call-done = bf16[8192,2048]{1,0:T(8,128)(2,1)} async-done(((bf16[2048,2048]{1,0:T(8,128)(2,1)}), bf16[8192,2048]{1,0:T(8,128)(2,1)}) %all-gather.24.cloned.1.call-update) | async-done | bytes 33554448 | tf_op jit(solution)/shard_map/all_gather | solution.py:255
  1724.6 21.7 convert_reduce_fusion.1
  1746.4 22.1 convert_reduce_fusion
  1768.5 27.0 fusion.207
  1795.5 37.4 %add_convert_fusion.1 = bf16[2048,8192]{1,0:T(8,128)(2,1)} fusion(f32[2048,8192]{1,0:T(8,128)} %fusion.207, bf16[256,8192]{1,0:T(8,128)(2,1)} %get-tuple-element.162, f32[256]{0:T(256)S(1)} %copy-done.110, f32[256]{0:T(256)S(1)} %copy-done.107, f32[2048]{0:T(1024)S(1)} %bitcast.481, f32[2048]{0:T(1024)S(1)} %bitcast.469, ...), kind=kOutput, calls=%fused_computation.1 | convolution fusion | flops 8626634752 | bytes 105924608 | tf_op jit(solution)/shard_map/dot_general | solution.py:13
  1833.0 30.1 fusion.192
  1863.0 39.8 %add_convert_fusion = bf16[8192,2048]{1,0:T(8,128)(2,1)} fusion(f32[8192,2048]{1,0:T(8,128)} %fusion.192, f32[256]{0:T(256)S(1)} %copy-done.154, bf16[1,2,256,2048]{3,2,1,0:T(8,128)(2,1)} %param.15, f32[256,8192]{1,0:T(8,128)} %convolution_add_fusion), kind=kOutput, calls=%fused_computation | convolution fusion | flops 8643936256 | bytes 110101504 | tf_op jit(solution)/shard_map/dot_general | solution.py:13
  1980.3 59.7 %reduce-scatter.21.cloned.1.call-done = bf16[512,6144]{1,0:T(8,128)(2,1)} async-done(((bf16[2048,6144]{1,0:T(8,128)(2,1)}), bf16[512,6144]{1,0:T(8,128)(2,1)}) %reduce-scatter.21.cloned.1.call-update) | async-done | bytes 6291472 | tf_op jit(solution)/shard_map/reduce_scatter | solution.py:275
  2040.0 291.6 %reduce-scatter.25.cloned.1.call-done = bf16[512,8192]{1,0:T(8,128)(2,1)} async-done(((bf16[2048,8192]{1,0:T(8,128)(2,1)}), bf16[512,8192]{1,0:T(8,128)(2,1)}) %reduce-scatter.25.cloned.1.call-update) | async-done | bytes 8388624
  2331.6 291.9 %reduce-scatter.27.cloned.1.call-done = bf16[2048,2048]{1,0:T(8,128)(2,1)} async-done(((bf16[8192,2048]{1,0:T(8,128)(2,1)}), bf16[2048,2048]{1,0:T(8,128)(2,1)}) %reduce-scatter.27.cloned.1.call-update) | async-done | bytes 8388624
  2711.4 29.8 all-reduce.7
  2746.6 373.5 %all-reduce.12.cloned.1.call-done = (bf16[512,6144]{1,0:T(8,128)(2,1)}, bf16[512,2048]{1,0:T(8,128)(2,1)}, bf16[512,8192]{1,0:T(8,128)(2,1)}, bf16[2048,2048]{1,0:T(8,128)(2,1)}) async-done(((bf16[512,6144]{1,0:T(8,128)(2,1)}, bf16[512,2048]{1,0:T(8,128)(2,1)}, bf16[512,8192]{1,0:T(8,128)(2,1)}, bf16[2048,2048]{1,0:T(8,128)(2,1)}), (bf16[512,6144]{1,0:T(8,128)(2,1)}, bf16[512,2048]{1,0:T(8,128)(2,1)}, ...) | async-done | bytes 25165840 | tf_op jit(solution)/shard_map/psum | solution.py:303
  (643 shorter events, 726.3 us)
Async XLA Ops:
  7.2 233.2 %all-gather.14.cloned.1.call-start = ((), (), s32[]{:S(2)}) async-start(), calls=%async_computation.8 | async-start | bytes 31457280 | tf_op jit(solution)/shard_map/all_gather | solution.py:249
  8.0 322.0 %all-gather.20.cloned.1.call-start = ((), (), s32[]{:S(2)}) async-start(), calls=%async_computation.11 | async-start | bytes 10485760 | tf_op jit(solution)/shard_map/all_gather | solution.py:251
  8.7 403.6 %all-gather.16.cloned.1.call-start = ((), (), s32[]{:S(2)}) async-start(), calls=%async_computation.9 | async-start | bytes 5242880 | tf_op jit(solution)/shard_map/all_gather | solution.py:84
  18.3 237.9 %copy-start.39 = (f32[4,1,512]{2,1,0:T(1,128)}, f32[4,1,512]{2,1,0:T(1,128)S(1)}, u32[]{:S(2)}) copy-start(f32[4,1,512]{2,1,0:T(1,128)S(1)} %convert_element_type.392) | copy-start | bytes 24580
  26.4 229.8 %copy-start.42 = (f32[4,1,512]{2,1,0:T(1,128)}, f32[4,1,512]{2,1,0:T(1,128)S(1)}, u32[]{:S(2)}) copy-start(f32[4,1,512]{2,1,0:T(1,128)S(1)} %convert_element_type.393) | copy-start | bytes 24580
  34.2 218.1 %copy-start.80 = (f32[256]{0:T(256)}, f32[256]{0:T(256)S(1)}, u32[]{:S(2)}) copy-start(f32[256]{0:T(256)S(1)} %get-tuple-element.164) | copy-start | bytes 3076
  34.2 222.0 %copy-start.106 = (f32[256]{0:T(256)}, f32[256]{0:T(256)S(1)}, u32[]{:S(2)}) copy-start(f32[256]{0:T(256)S(1)} %get-tuple-element.163) | copy-start | bytes 3076
  34.9 217.4 %copy-start.99 = (f32[256]{0:T(256)}, f32[256]{0:T(256)S(1)}, u32[]{:S(2)}) copy-start(f32[256]{0:T(256)S(1)} %add_rsqrt_fusion.1) | copy-start | bytes 3076
  256.1 237.5 %all-gather.26.cloned.1.call-start = ((), (), s32[]{:S(2)}) async-start(), calls=%async_computation.14 | async-start | bytes 5242880 | tf_op jit(solution)/shard_map/all_gather | solution.py:84
  271.9 302.2 %all-gather.18.cloned.1.call-start = ((), (), s32[]{:S(2)}) async-start(), calls=%async_computation.10 | async-start | bytes 5242880 | tf_op jit(solution)/shard_map/all_gather | solution.py:83
  286.2 368.8 %all-gather.28.cloned.1.call-start = ((), (), s32[]{:S(2)}) async-start(), calls=%async_computation.15 | async-start | bytes 5242880 | tf_op jit(solution)/shard_map/all_gather | solution.py:83
  304.6 696.4 %reduce-scatter.13.cloned.1.call-start = ((), (), s32[]{:S(2)}) async-start(), calls=%async_computation.16 | async-start | bytes 5242880 | tf_op jit(solution)/shard_map/reduce_scatter | solution.py:186
  782.4 222.5 %reduce-scatter.17.cloned.1.call-start = ((), (), s32[]{:S(2)}) async-start(), calls=%async_computation.18 | async-start | bytes 5242880 | tf_op jit(solution)/shard_map/reduce_scatter | solution.py:186
  891.2 154.7 %reduce-scatter.15.cloned.1.call-start = ((), (), s32[]{:S(2)}) async-start(), calls=%async_computation.17 | async-start | bytes 5242880 | tf_op jit(solution)/shard_map/reduce_scatter | solution.py:189
  910.7 215.3 %reduce-scatter.19.cloned.1.call-start = ((), (), s32[]{:S(2)}) async-start(), calls=%async_computation.19 | async-start | bytes 5242880 | tf_op jit(solution)/shard_map/reduce_scatter | solution.py:189
  930.5 495.1 %all-gather.22.cloned.1.call-start = ((), (), s32[]{:S(2)}) async-start(), calls=%async_computation.12 | async-start | bytes 41943040 | tf_op jit(solution)/shard_map/all_gather | solution.py:253
  931.3 793.4 %all-gather.24.cloned.1.call-start = ((), (), s32[]{:S(2)}) async-start(), calls=%async_computation.13 | async-start | bytes 41943040 | tf_op jit(solution)/shard_map/all_gather | solution.py:255
  931.9 1048.4 %reduce-scatter.23.cloned.1.call-start = ((), (), s32[]{:S(2)}) async-start(), calls=%async_computation.21 | async-start | bytes 10485760 | tf_op jit(solution)/shard_map/reduce_scatter | solution.py:281
  979.9 1060.1 %reduce-scatter.21.cloned.1.call-start = ((), (), s32[]{:S(2)}) async-start(), calls=%async_computation.20 | async-start | bytes 31457280 | tf_op jit(solution)/shard_map/reduce_scatter | solution.py:275
  1158.0 1173.6 %reduce-scatter.25.cloned.1.call-start = ((), (), s32[]{:S(2)}) async-start(), calls=%async_computation.22 | async-start | bytes 41943040
  1447.3 277.3 %copy-start.157 = (f32[256]{0:T(256)S(1)}, f32[256]{0:T(256)}, u32[]{:S(2)}) copy-start(f32[256]{0:T(256)} %copy-done.155) | copy-start | bytes 3076
  1832.9 790.5 %reduce-scatter.27.cloned.1.call-start = ((), (), s32[]{:S(2)}) async-start(), calls=%async_computation.23 | async-start | bytes 41943040
  1902.9 1217.2 %all-reduce.12.cloned.1.call-start = ((), (), s32[]{:S(2)}) async-start(), calls=%async_computation.24 | async-start | bytes 50331648 | tf_op jit(solution)/shard_map/psum | solution.py:303
  2742.4 410.4 %copy-start.158 = (f32[512]{0:T(512)}, f32[512]{0:T(512)S(1)}, u32[]{:S(2)}) copy-start(f32[512]{0:T(512)S(1)} %convert_element_type.381) | copy-start | bytes 6148
  (187 other events, 2263.9 us)
Sparse Core Ops, SparseCore 0:
  9.9 230.4 all-gather.13
  242.3 87.6 all-gather.19
  331.5 80.7 all-gather.15
  414.3 79.2 all-gather.25
  495.0 79.0 all-gather.17
  576.2 78.7 all-gather.27
  782.5 74.9 reduce-scatter.12
  891.3 74.8 reduce-scatter.16
  968.6 77.2 reduce-scatter.14
  1048.7 77.2 reduce-scatter.18
  1127.8 297.7 all-gather.21
  1427.4 297.2 all-gather.23
  1728.2 86.4 reduce-scatter.22
  1818.0 221.9 reduce-scatter.20
  2042.9 288.6 reduce-scatter.24
  2334.8 288.6 reduce-scatter.26
  2626.2 493.8 all-reduce.11
where the time goes:
time: 3170 us; the launch traced here: 3160 us
  waiting for transfers between devices  2120 us (67%)
  matrix products  665 us (21%)
  other arithmetic  161 us (5%)
  local copies, waits for them, and re-layouts  95.3 us (3%)
  blocking collectives  93.9 us (3%)
    unnamed x19, waiting for transfers between devices  586 us
    psum x1, waiting for transfers between devices, body(): lax.psum(summed[2].astype(jnp.bfloat16), ('dp', 'ctx')).astype(jnp.float32)  374 us
    all_gather x1, waiting for transfers between devices, body(): lax.all_gather(w_up, 'fsdp', axis=0, tiled=True)  259 us
    all_gather x1, waiting for transfers between devices, body(): lax.all_gather(w_down, 'fsdp', axis=0, tiled=True)  258 us
    dot_general x8, matrix products, contract_rows(): lax.dot_general(left, right, (((0,), (0,)), ((), ())), preferred_element_...  206 us
    all_gather x1, waiting for transfers between devices, body(): lax.all_gather(w_qkv, 'fsdp', axis=0, tiled=True)  206 us
    all_gather x2, waiting for transfers between devices, layer_step(): lax.all_gather(keyed, 'ctx', axis=0, tiled=True)  143 us
    all_gather x2, waiting for transfers between devices, layer_step(): lax.all_gather(valued, 'ctx', axis=0, tiled=True)  124 us
  transfers between devices with their start and end apart: 17, of which 14 were waited for; matrix products, arithmetic and copies ran while one was open for 24% of the time, Pallas kernels for 0%

commit v1 on v0

--- a/solution.py
+++ b/solution.py
@@ -300,7 +300,9 @@
     totals = (
         lax.psum(summed[0].astype(jnp.bfloat16), ("dp", "ctx")).astype(jnp.float32),
         lax.psum(summed[1].astype(jnp.bfloat16), ("dp", "ctx")).astype(jnp.float32),
-        lax.psum(summed[2].astype(jnp.bfloat16), ("dp", "ctx")).astype(jnp.float32),
+        jnp.sum(lax.all_gather(summed[2].astype(jnp.bfloat16), ("dp", "ctx")), axis=0).astype(
+            jnp.float32
+        ),
         lax.psum(summed[3].astype(jnp.bfloat16), ("dp", "ctx")).astype(jnp.float32),
         lax.psum(summed[4].astype(jnp.bfloat16), ("dp", "ctx")).astype(jnp.float32),
         lax.psum(summed[5].astype(jnp.bfloat16), ("dp", "ctx")).astype(jnp.float32),

time: 3170 us -> 3320 us (1.047)
  waiting for transfers between devices: 2120 us -> 2250 us
  other arithmetic: 161 us -> 195 us
    all_gather x0 -> x1, waiting for transfers between devices: none -> 396 us  [body(): lax.all_gather(summed[2].astype(jnp.bfloat16), ('dp', 'ctx'))]
    all_gather x1, waiting for transfers between devices: 259 us -> 0.02 us  [body(): lax.all_gather(w_up, 'fsdp', axis=0, tiled=True)]
    psum x1, waiting for transfers between devices: 374 us -> 178 us  [body(): lax.psum(summed[4].astype(jnp.bfloat16), ('dp', 'ctx')).astype(jnp.float32)]
    reduce_scatter x1, waiting for transfers between devices: 59.7 us -> 225 us  [body(): lax.psum_scatter(summed[2].astype(jnp.bfloat16), 'fsdp', scatter_dimensio...]
    reduce_scatter x1, waiting for transfers between devices: 0.01 us -> 62.7 us  [body(): lax.psum_scatter(summed[4].astype(jnp.bfloat16), 'fsdp', scatter_dimensio...]
    all_gather x1, waiting for transfers between devices: 258 us -> 219 us  [body(): lax.all_gather(w_down, 'fsdp', axis=0, tiled=True)]
    unnamed x19 -> x20, waiting for transfers between devices: 586 us -> 586 us
  transfers between devices with their start and end apart: 17 -> 18, of which waited for: 14 -> 15; matrix products, arithmetic and copies ran while one was open for 24% -> 27% of each run, Pallas kernels for 0% -> 0%
where the time goes in v1:
time: 3320 us; the launch traced here: 3310 us
  waiting for transfers between devices  2250 us (68%)
  matrix products  657 us (20%)
  other arithmetic  195 us (6%)
  local copies, waits for them, and re-layouts  94.3 us (3%)
  blocking collectives  94.3 us (3%)
    unnamed x20, waiting for transfers between devices  586 us
    all_gather x1, waiting for transfers between devices, body(): lax.all_gather(summed[2].astype(jnp.bfloat16), ('dp', 'ctx'))  396 us
    reduce_scatter x1, waiting for transfers between devices, body(): lax.psum_scatter(summed[2].astype(jnp.bfloat16), 'fsdp', scatter_dimensio...  225 us
    all_gather x1, waiting for transfers between devices, body(): lax.all_gather(w_down, 'fsdp', axis=0, tiled=True)  219 us
    all_gather x1, waiting for transfers between devices, body(): lax.all_gather(w_qkv, 'fsdp', axis=0, tiled=True)  206 us
    dot_general x8, matrix products, contract_rows(): lax.dot_general(left, right, (((0,), (0,)), ((), ())), preferred_element_...  198 us
    psum x1, waiting for transfers between devices, body(): lax.psum(summed[4].astype(jnp.bfloat16), ('dp', 'ctx')).astype(jnp.float32)  178 us
    all_gather x2, waiting for transfers between devices, layer_step(): lax.all_gather(keyed, 'ctx', axis=0, tiled=True)  139 us
  transfers between devices with their start and end apart: 18, of which 15 were waited for; matrix products, arithmetic and copies ran while one was open for 27% of the time, Pallas kernels for 0%

profile of v1, /device:TPU:0, one launch (start us, length us, event | category | flops | bytes accessed | tf_op | source)
XLA Modules:
  0.0 3313.4 jit_solution(4452613626124083830)
XLA Ops:
  34.8 205.6 %all-gather.16.cloned.1.call-done = bf16[2048,6144]{1,0:T(8,128)(2,1)} async-done(((bf16[512,6144]{1,0:T(8,128)(2,1)}), bf16[2048,6144]{1,0:T(8,128)(2,1)}) %all-gather.16.cloned.1.call-update) | async-done | bytes 25165840 | tf_op jit(solution)/shard_map/all_gather | solution.py:249
  305.7 24.2 all-gather.22.cloned.1.call-done
  358.3 54.5 %all-gather.28.cloned.1.call-done = bf16[1024,2048]{1,0:T(8,128)(2,1)} async-done(((bf16[256,2048]{1,0:T(8,128)(2,1)}), bf16[1024,2048]{1,0:T(8,128)(2,1)}) %all-gather.28.cloned.1.call-update) | async-done | bytes 4194320 | tf_op jit(solution)/shard_map/all_gather | solution.py:84
  424.1 69.5 %all-gather.18.cloned.1.call-done = bf16[1024,2048]{1,0:T(8,128)(2,1)} async-done(((bf16[256,2048]{1,0:T(8,128)(2,1)}), bf16[1024,2048]{1,0:T(8,128)(2,1)}) %all-gather.18.cloned.1.call-update) | async-done | bytes 4194320 | tf_op jit(solution)/shard_map/all_gather | solution.py:84
  504.7 70.0 %all-gather.30.cloned.1.call-done = bf16[1024,2048]{0,1:T(8,128)(2,1)} async-done(((bf16[256,2048]{0,1:T(8,128)(2,1)}), bf16[1024,2048]{0,1:T(8,128)(2,1)}) %all-gather.30.cloned.1.call-update) | async-done | bytes 4194320 | tf_op jit(solution)/shard_map/all_gather | solution.py:83
  586.4 69.1 %all-gather.20.cloned.1.call-done = bf16[1024,2048]{0,1:T(8,128)(2,1)} async-done(((bf16[256,2048]{0,1:T(8,128)(2,1)}), bf16[1024,2048]{0,1:T(8,128)(2,1)}) %all-gather.20.cloned.1.call-update) | async-done | bytes 4194320 | tf_op jit(solution)/shard_map/all_gather | solution.py:83
  774.5 29.8 multiply_convert_fusion.3
  849.5 26.6 multiply_convert_fusion.7
  1032.7 219.3 %all-gather.26.cloned.1.call-done = bf16[8192,2048]{1,0:T(8,128)(2,1)} async-done(((bf16[2048,2048]{1,0:T(8,128)(2,1)}), bf16[8192,2048]{1,0:T(8,128)(2,1)}) %all-gather.26.cloned.1.call-update) | async-done | bytes 33554448 | tf_op jit(solution)/shard_map/all_gather | solution.py:255
  1273.7 21.9 convert_reduce_fusion.1
  1295.7 25.7 fusion.207
  1321.4 34.8 %add_convert_fusion.1 = bf16[2048,8192]{1,0:T(8,128)(2,1)} fusion(f32[2048,8192]{1,0:T(8,128)} %fusion.207, bf16[256,8192]{1,0:T(8,128)(2,1)} %get-tuple-element.161, f32[256]{0:T(256)S(1)} %copy-done.104, f32[256]{0:T(256)S(1)} %copy-done.102, f32[2048]{0:T(1024)S(1)} %bitcast.475, f32[2048]{0:T(1024)S(1)} %bitcast.465, ...), kind=kOutput, calls=%fused_computation.1 | convolution fusion | flops 8626634752 | bytes 105924608 | tf_op jit(solution)/shard_map/dot_general | solution.py:13
  1356.2 27.8 fusion.192
  1384.0 38.3 %add_convert_fusion = bf16[8192,2048]{1,0:T(8,128)(2,1)} fusion(f32[8192,2048]{1,0:T(8,128)} %fusion.192, f32[256]{0:T(256)S(1)} %copy-done.140, bf16[1,2,256,2048]{3,2,1,0:T(8,128)(2,1)} %param.15, f32[256,8192]{1,0:T(8,128)} %convolution_add_fusion), kind=kOutput, calls=%fused_computation | convolution fusion | flops 8643936256 | bytes 110101504 | tf_op jit(solution)/shard_map/dot_general | solution.py:13
  1459.4 30.8 reduce-scatter.15.cloned.1.call-done
  1510.9 59.5 %reduce-scatter.19.cloned.1.call-done = bf16[256,2048]{0,1:T(8,128)(2,1)} async-done(((bf16[1024,2048]{0,1:T(8,128)(2,1)}), bf16[256,2048]{0,1:T(8,128)(2,1)}) %reduce-scatter.19.cloned.1.call-update) | async-done | bytes 1048592 | tf_op jit(solution)/shard_map/reduce_scatter | solution.py:189
  1570.4 27.8 add_convert_fusion.2
  1598.2 62.7 %reduce-scatter.23.cloned.1.call-done = bf16[512,2048]{1,0:T(8,128)(2,1)} async-done(((bf16[2048,2048]{1,0:T(8,128)(2,1)}), bf16[512,2048]{1,0:T(8,128)(2,1)}) %reduce-scatter.23.cloned.1.call-update) | async-done | bytes 2097168 | tf_op jit(solution)/shard_map/reduce_scatter | solution.py:281
  1660.9 291.9 %reduce-scatter.25.cloned.1.call-done = bf16[512,8192]{1,0:T(8,128)(2,1)} async-done(((bf16[2048,8192]{1,0:T(8,128)(2,1)}), bf16[512,8192]{1,0:T(8,128)(2,1)}) %reduce-scatter.25.cloned.1.call-update) | async-done | bytes 8388624
  1952.8 291.6 %reduce-scatter.27.cloned.1.call-done = bf16[2048,2048]{1,0:T(8,128)(2,1)} async-done(((bf16[8192,2048]{1,0:T(8,128)(2,1)}), bf16[2048,2048]{1,0:T(8,128)(2,1)}) %reduce-scatter.27.cloned.1.call-update) | async-done | bytes 8388624
  2244.5 225.1 %reduce-scatter.21.cloned.1.call-done = bf16[512,6144]{1,0:T(8,128)(2,1)} async-done(((bf16[2048,6144]{1,0:T(8,128)(2,1)}), bf16[512,6144]{1,0:T(8,128)(2,1)}) %reduce-scatter.21.cloned.1.call-update) | async-done | bytes 6291472 | tf_op jit(solution)/shard_map/reduce_scatter | solution.py:275
  2633.4 29.8 all-reduce.7
  2668.9 178.2 %all-reduce.12.cloned.1.call-done = (bf16[512,2048]{1,0:T(8,128)(2,1)}, bf16[512,8192]{1,0:T(8,128)(2,1)}, bf16[2048,2048]{1,0:T(8,128)(2,1)}) async-done(((bf16[512,2048]{1,0:T(8,128)(2,1)}, bf16[512,8192]{1,0:T(8,128)(2,1)}, bf16[2048,2048]{1,0:T(8,128)(2,1)}), (bf16[512,2048]{1,0:T(8,128)(2,1)}, bf16[512,8192]{1,0:T(8,128)(2,1)}, bf16[2048,2048]{1,0:T(8,128)(2,1)})) %all-reduce.12.cloned.1.call-update) | async-done | bytes 18874384 | tf_op jit(solution)/shard_map/psum | solution.py:307
  2880.5 395.5 %all-gather.32.cloned.1.call-done = bf16[4096,6144]{1,0:T(8,128)(2,1)} async-done(((bf16[512,6144]{1,0:T(8,128)(2,1)}), bf16[4096,6144]{1,0:T(8,128)(2,1)}) %all-gather.32.cloned.1.call-update) | async-done | bytes 50331664 | tf_op jit(solution)/shard_map/all_gather | solution.py:303
  (604 shorter events, 784.0 us)
Async XLA Ops:
  7.2 233.2 %all-gather.16.cloned.1.call-start = ((), (), s32[]{:S(2)}) async-start(), calls=%async_computation.8 | async-start | bytes 31457280 | tf_op jit(solution)/shard_map/all_gather | solution.py:249
  8.0 321.9 %all-gather.22.cloned.1.call-start = ((), (), s32[]{:S(2)}) async-start(), calls=%async_computation.11 | async-start | bytes 10485760 | tf_op jit(solution)/shard_map/all_gather | solution.py:251
  8.7 404.1 %all-gather.28.cloned.1.call-start = ((), (), s32[]{:S(2)}) async-start(), calls=%async_computation.14 | async-start | bytes 5242880 | tf_op jit(solution)/shard_map/all_gather | solution.py:84
  26.5 229.6 %copy-start.39 = (f32[4,1,512]{2,1,0:T(1,128)}, f32[4,1,512]{2,1,0:T(1,128)S(1)}, u32[]{:S(2)}) copy-start(f32[4,1,512]{2,1,0:T(1,128)S(1)} %convert_element_type.395) | copy-start | bytes 24580
  256.0 237.5 %all-gather.18.cloned.1.call-start = ((), (), s32[]{:S(2)}) async-start(), calls=%async_computation.9 | async-start | bytes 5242880 | tf_op jit(solution)/shard_map/all_gather | solution.py:84
  271.8 302.9 %all-gather.30.cloned.1.call-start = ((), (), s32[]{:S(2)}) async-start(), calls=%async_computation.15 | async-start | bytes 5242880 | tf_op jit(solution)/shard_map/all_gather | solution.py:83
  285.9 369.6 %all-gather.20.cloned.1.call-start = ((), (), s32[]{:S(2)}) async-start(), calls=%async_computation.10 | async-start | bytes 5242880 | tf_op jit(solution)/shard_map/all_gather | solution.py:83
  299.6 697.6 %all-gather.24.cloned.1.call-start = ((), (), s32[]{:S(2)}) async-start(), calls=%async_computation.12 | async-start | bytes 41943040 | tf_op jit(solution)/shard_map/all_gather | solution.py:253
  300.3 951.7 %all-gather.26.cloned.1.call-start = ((), (), s32[]{:S(2)}) async-start(), calls=%async_computation.13 | async-start | bytes 41943040 | tf_op jit(solution)/shard_map/all_gather | solution.py:255
  301.1 1143.2 %reduce-scatter.17.cloned.1.call-start = ((), (), s32[]{:S(2)}) async-start(), calls=%async_computation.18 | async-start | bytes 5242880 | tf_op jit(solution)/shard_map/reduce_scatter | solution.py:186
  358.3 301.1 %copy-start.53 = (bf16[256,512]{0,1:T(8,128)(2,1)}, bf16[256,512]{0,1:T(8,128)(2,1)S(1)}, u32[]{:S(2)}) copy-start(bf16[256,512]{0,1:T(8,128)(2,1)S(1)} %get-tuple-element.112) | copy-start | bytes 786436
  817.5 631.4 %reduce-scatter.13.cloned.1.call-start = ((), (), s32[]{:S(2)}) async-start(), calls=%async_computation.16 | async-start | bytes 5242880 | tf_op jit(solution)/shard_map/reduce_scatter | solution.py:186
  889.2 601.0 %reduce-scatter.15.cloned.1.call-start = ((), (), s32[]{:S(2)}) async-start(), calls=%async_computation.17 | async-start | bytes 5242880 | tf_op jit(solution)/shard_map/reduce_scatter | solution.py:189
  908.8 661.5 %reduce-scatter.19.cloned.1.call-start = ((), (), s32[]{:S(2)}) async-start(), calls=%async_computation.19 | async-start | bytes 5242880 | tf_op jit(solution)/shard_map/reduce_scatter | solution.py:189
  949.9 711.1 %reduce-scatter.23.cloned.1.call-start = ((), (), s32[]{:S(2)}) async-start(), calls=%async_computation.21 | async-start | bytes 10485760 | tf_op jit(solution)/shard_map/reduce_scatter | solution.py:281
  996.6 956.1 %reduce-scatter.25.cloned.1.call-start = ((), (), s32[]{:S(2)}) async-start(), calls=%async_computation.23 | async-start | bytes 41943040
  1356.1 888.3 %reduce-scatter.27.cloned.1.call-start = ((), (), s32[]{:S(2)}) async-start(), calls=%async_computation.24 | async-start | bytes 41943040
  1422.4 1047.2 %reduce-scatter.21.cloned.1.call-start = ((), (), s32[]{:S(2)}) async-start(), calls=%async_computation.20 | async-start | bytes 31457280 | tf_op jit(solution)/shard_map/reduce_scatter | solution.py:275
  1598.2 1248.9 %all-reduce.12.cloned.1.call-start = ((), (), s32[]{:S(2)}) async-start(), calls=%async_computation.25 | async-start | bytes 37748736 | tf_op jit(solution)/shard_map/psum | solution.py:307
  2244.4 233.1 %copy-start.152 = (bf16[512]{0:T(512)(128)(2,1)S(1)}, bf16[512]{0:T(512)(128)(2,1)}, u32[]{:S(2)}) copy-start(bf16[512]{0:T(512)(128)(2,1)} %param.27) | copy-start | bytes 3076
  2244.4 240.4 %copy-start.153 = (u32[32]{0:T(128)S(1)}, u32[32]{0:T(128)}, u32[]{:S(2)}) copy-start(u32[32]{0:T(128)} %constant.66) | copy-start | bytes 388
  2244.4 242.9 %copy-start.90 = (bf16[8,64,256]{2,1,0:T(8,128)(2,1)S(1)}, bf16[8,64,256]{2,1,0:T(8,128)(2,1)}, u32[]{:S(2)}) copy-start(bf16[8,64,256]{2,1,0:T(8,128)(2,1)} %copy-done.89) | copy-start | bytes 786436
  2244.4 1031.7 %all-gather.32.cloned.1.call-start = ((), (), s32[]{:S(2)}) async-start(), calls=%async_computation.22 | async-start | bytes 56623104 | tf_op jit(solution)/shard_map/all_gather | solution.py:303
  2665.0 640.5 %copy-start.144 = (f32[512]{0:T(512)}, f32[512]{0:T(512)S(1)}, u32[]{:S(2)}) copy-start(f32[512]{0:T(512)S(1)} %convert_element_type.383) | copy-start | bytes 6148
  (168 other events, 2675.1 us)
Sparse Core Ops, SparseCore 0:
  9.9 230.4 all-gather.15
  242.2 87.6 all-gather.21
  332.0 80.7 all-gather.27
  414.3 79.2 all-gather.17
  495.6 79.0 all-gather.29
  576.7 78.7 all-gather.19
  657.3 295.5 all-gather.23
  954.7 297.2 all-gather.25
  1254.3 76.7 reduce-scatter.16
  1333.3 77.2 reduce-scatter.12
  1412.9 77.2 reduce-scatter.14
  1493.0 77.2 reduce-scatter.18
  1574.0 86.8 reduce-scatter.22
  1664.1 288.6 reduce-scatter.24
  1955.7 288.6 reduce-scatter.26
  2247.7 221.8 reduce-scatter.20
  2472.2 374.8 all-reduce.11
  2848.5 427.5 all-gather.31
